TPU v7x, 256 devices: a whole 4x4x8 slice. The times are simulated.
256 devices in a mesh: seq: 64 (over z, x, core), tp: 4 (over y).
Axes of the slice: x: 4, y: 4, z: 8, core: 2. Of those that a mesh axis runs over, the one named last changes fastest.
Arguments:
- layer_input: bfloat16 [16384, 2048], P('seq'), may hold values from -1.5 to 1.5
- norm_gain: float32 [2048], replicated, may hold values from 0.5 to 1.5
- w_query: bfloat16 [2048, 2048], P(None, 'tp')
- key_weight: bfloat16 [2048, 1024], P(None, 'tp')
- value_weight: bfloat16 [2048, 1024], P(None, 'tp'), may hold values from -0.125 to 0.125
- w_out: bfloat16 [2048, 2048], P('tp'), may hold values from -1 to 1
- query_gain: float32 [128], replicated, may hold values from 0.6 to 6, as said below
- key_gain: float32 [128], replicated, may hold values from 0.6 to 6, as said below
- seg_ids: int32 [16384], P('seq'), may hold values from 0 to 7, as said below
- positions: int32 [16384], P('seq'), may hold values from 0 to 13106, as said below
- post_gain: float32 [2048], replicated, may hold values from 0.5 to 1.5
- w_gate: bfloat16 [2048, 3072], P('seq', 'tp'), may hold values from -0.125 to 0.125
- w_up: bfloat16 [2048, 3072], P('seq', 'tp'), may hold values from -0.125 to 0.125
- w_down: bfloat16 [3072, 2048], P('tp', 'seq'), may hold values from -0.21875 to 0.21875
Outputs:
- hidden: bfloat16 [16384, 2048], P('seq')
- key_cache: bfloat16 [16384, 1024], P('seq', 'tp')
- value_cache: bfloat16 [16384, 1024], P('seq', 'tp')
Inputs may be any that keep to these rules, and one draw needn't show every extreme that they name: `seg_ids`: prompt numbers never fall along the stream; each of the 8 prompts is a contiguous run of one or more tokens, and one prompt has exactly 13107 tokens. `positions`: each token's place in its prompt, counting from 0 at the prompt's first token. `query_gain`: positive gains. `key_gain`: positive gains.
All inputs are finite; a program needn't handle non-finite values.
Results may differ from a plain program's by a relative error of at most 0.02.
Values may be sent and summed in bfloat16 or wider, within the bound.
A program may use at most 128 MiB of HBM per device.

v0:
```python
import math
import jax
import jax.numpy as jnp
from jax import lax
from jax.sharding import PartitionSpec as P


def rms(v, gain):
    return v * lax.rsqrt(jnp.mean(v * v, axis=-1, keepdims=True) + 1e-06) * gain


def rope(v, place):
    half = v.shape[-1] // 2
    freqs = 1000000.0 ** (-2.0 * jnp.arange(half, dtype=jnp.float32) / v.shape[-1])
    angle = place.astype(jnp.float32)[:, None] * freqs[None, :]
    cosine = jnp.cos(angle)[:, None, :]
    sine = jnp.sin(angle)[:, None, :]
    block_start = v[..., :half]
    second = v[..., half:]
    return jnp.concatenate(
        [block_start * cosine - second * sine, second * cosine + block_start * sine], axis=-1
    )


def body(
    layer_input,
    norm_gain,
    w_query,
    key_weight,
    value_weight,
    w_out,
    query_gain,
    key_gain,
    seg_ids,
    positions,
    post_gain,
    w_gate,
    w_up,
    w_down,
):
    rows = layer_input.shape[0]
    head_size = query_gain.shape[0]
    query_local = w_query.shape[1] // head_size
    kv_local = key_weight.shape[1] // head_size
    head_group = query_local // kv_local
    scale = 1.0 / math.sqrt(head_size)
    xf = layer_input.astype(jnp.float32)
    normed_input = rms(xf, norm_gain).astype(jnp.bfloat16)
    query_matrix = jnp.dot(normed_input, w_query, preferred_element_type=jnp.float32).reshape(
        rows, query_local, head_size
    )
    query_matrix = rope(rms(query_matrix, query_gain), positions).astype(jnp.bfloat16)
    key_matrix = jnp.dot(normed_input, key_weight, preferred_element_type=jnp.float32).reshape(
        rows, kv_local, head_size
    )
    key_matrix = rope(rms(key_matrix, key_gain), positions).astype(jnp.bfloat16)
    key_cache = key_matrix.reshape(rows, kv_local * head_size)
    value_cache = jnp.dot(normed_input, value_weight, preferred_element_type=jnp.float32).astype(
        jnp.bfloat16
    )
    grouped = query_matrix.reshape(rows, kv_local, head_group, head_size).transpose(1, 2, 0, 3)
    me = lax.axis_index("seq")
    my_last = me * rows + rows - 1

    def update(state, key_rows, value_rows, seg_rows, place_rows):
        top, total, acc = state
        count = key_rows.shape[0]
        s = (
            jnp.einsum(
                "hgqd,khd->hgqk",
                grouped,
                key_rows.reshape(count, kv_local, head_size),
                preferred_element_type=jnp.float32,
            )
            * scale
        )
        allowed = (seg_ids[:, None] == seg_rows[None, :]) & (
            place_rows[None, :] <= positions[:, None]
        )
        s = jnp.where(allowed, s, -1e30)
        new_top = jnp.maximum(top, jnp.max(s, axis=-1))
        p = jnp.where(allowed, jnp.exp(s - new_top[..., None]), 0.0)
        decay = jnp.exp(top - new_top)
        total = total * decay + jnp.sum(p, axis=-1)
        acc = acc * decay[..., None] + jnp.einsum(
            "hgqk,khd->hgqd",
            p.astype(jnp.bfloat16),
            value_rows.reshape(count, kv_local, head_size),
            preferred_element_type=jnp.float32,
        )
        return (new_top, total, acc)

    start_state = (
        jnp.full((kv_local, head_group, rows), -1e30, jnp.float32),
        jnp.zeros((kv_local, head_group, rows), jnp.float32),
        jnp.zeros((kv_local, head_group, rows, head_size), jnp.float32),
    )
    travel = (key_cache, value_cache, seg_ids, positions)
    dead = jnp.int32(0) < 0
    key_rows = lax.all_gather(travel[0], "seq", axis=0, tiled=True)
    value_rows = lax.all_gather(travel[1], "seq", axis=0, tiled=True)
    seg_rows = lax.all_gather(travel[2], "seq", axis=0, tiled=True)
    place_rows = lax.all_gather(travel[3], "seq", axis=0, tiled=True)
    count = key_rows.shape[0]
    shards = count // rows
    limit = max(1, 1024 // rows)
    factor = 1
    for trial in range(1, limit + 1):
        if shards % trial == 0:
            factor = trial
    width = rows * factor

    def one_block(step, inner):
        offset = step * width
        kb = lax.dynamic_slice_in_dim(key_rows, offset, width, 0)
        vb = lax.dynamic_slice_in_dim(value_rows, offset, width, 0)
        sb = lax.dynamic_slice_in_dim(seg_rows, offset, width, 0)
        pb = lax.dynamic_slice_in_dim(place_rows, offset, width, 0)
        skip = dead | (offset > my_last) | (sb[width - 1] < seg_ids[0])
        return lax.cond(skip, lambda c: c, lambda c: update(c, kb, vb, sb, pb), inner)

    top, total, acc = lax.fori_loop(0, count // width, one_block, start_state)
    attended = (acc / total[..., None]).astype(jnp.bfloat16)
    attended = attended.transpose(2, 0, 1, 3).reshape(rows, query_local * head_size)
    partial_out = jnp.dot(attended, w_out, preferred_element_type=jnp.float32)
    summed = lax.psum(partial_out.astype(jnp.bfloat16), "tp").astype(jnp.float32)
    mid = (xf + summed).astype(jnp.bfloat16)
    mid_f = mid.astype(jnp.float32)
    post_normed = rms(mid_f, post_gain).astype(jnp.bfloat16)
    gate = jnp.dot(
        post_normed,
        lax.all_gather(w_gate, "seq", axis=0, tiled=True),
        preferred_element_type=jnp.float32,
    )
    up = jnp.dot(
        post_normed,
        lax.all_gather(w_up, "seq", axis=0, tiled=True),
        preferred_element_type=jnp.float32,
    )
    act = (jax.nn.silu(gate) * up).astype(jnp.bfloat16)
    terms = jnp.dot(
        act, lax.all_gather(w_down, "seq", axis=1, tiled=True), preferred_element_type=jnp.float32
    )
    ffn_total = lax.psum(terms.astype(jnp.bfloat16), "tp").astype(jnp.float32)
    hidden = (mid_f + ffn_total).astype(jnp.bfloat16)
    return (hidden, key_cache, value_cache)


def solution(mesh):
    in_specs = (
        P("seq", None),
        P(),
        P(None, "tp"),
        P(None, "tp"),
        P(None, "tp"),
        P("tp", None),
        P(),
        P(),
        P("seq"),
        P("seq"),
        P(),
        P("seq", "tp"),
        P("seq", "tp"),
        P("tp", "seq"),
    )
    out_specs = (P("seq", None), P("seq", "tp"), P("seq", "tp"))
    return jax.shard_map(body, mesh=mesh, in_specs=in_specs, out_specs=out_specs, check_vma=False)
```

profile of v0, /device:TPU:2, one launch (start us, length us, event | category | flops | bytes accessed | tf_op | source)
XLA Modules:
  0.0 657.9 jit_solution(4688254087747547651)
XLA Ops:
  7.3 1.6 fusion.12
  8.9 3.0 multiply_reduce_fusion.1
  12.0 0.5 multiply_cosine_fusion
  12.7 1.0 multiply_multiply_fusion.1
  13.8 0.8 copy.77
  14.6 2.4 convolution_convert_fusion.2
  17.1 3.2 fusion.28
  20.3 1.2 reshape.128
  22.2 0.5 subtract_convert_fusion
  22.8 46.4 %all-gather = s32[64,1,256]{2,1,0:T(1,128)S(1)} all-gather(s32[1,1,256]{2,1,0:T(1,128)S(1)} %bitcast.61), channel_id=1, replica_groups=mesh['seq'=64,'tp'=4] {'seq'}, dimensions={0}, use_global_device_ids=true | all-gather | bytes 66560 | tf_op jit(solution)/shard_map/all_gather | solution.py:102
  69.2 41.5 %all-gather.1 = s32[64,1,256]{2,1,0:T(1,128)S(1)} all-gather(s32[1,1,256]{2,1,0:T(1,128)S(1)} %bitcast.60), channel_id=1, replica_groups=mesh['seq'=64,'tp'=4] {'seq'}, dimensions={0}, use_global_device_ids=true | all-gather | bytes 66560 | tf_op jit(solution)/shard_map/all_gather | solution.py:103
  110.9 11.9 %copy.67 = bf16[16384,256]{0,1:T(8,128)(2,1)} copy(bf16[16384,256]{1,0:T(8,128)(2,1)} %all-gather.8.cloned.1.call-done) | data formatting | bytes 16777216 | tf_op jit(solution)/shard_map/while | solution.py:122
  122.8 60.4 %all-gather.10.cloned.1.call-done = bf16[16384,256]{1,0:T(8,128)(2,1)} async-done(((bf16[256,256]{1,0:T(8,128)(2,1)}), bf16[16384,256]{1,0:T(8,128)(2,1)}) %all-gather.10.cloned.1.call-update) | async-done | bytes 8388624 | tf_op jit(solution)/shard_map/all_gather | solution.py:101
  183.2 11.8 %copy.68 = bf16[16384,256]{0,1:T(8,128)(2,1)} copy(bf16[16384,256]{1,0:T(8,128)(2,1)} %all-gather.10.cloned.1.call-done) | data formatting | bytes 16777216 | tf_op jit(solution)/shard_map/while | solution.py:122
  195.0 44.5 %while.17 = (s32[]{:T(128)}, f32[2,2,256]{2,1,0:T(2,128)S(1)}, f32[2,2,256]{2,1,0:T(2,128)S(1)}, f32[2,2,256,128]{3,2,1,0:T(8,128)S(1)}, s32[]{:T(128)}, /*index...) while((s32[]{:T(128)}, f32[2,2,256]{2,1,0:T(2,128)S(1)}, ...), condition=%wide.region_8.9_spmd, body=%wide.region_3.8_spmd.sunk | while | flops 551553024 | bytes 18180480 | solution.py:122
  195.1 0.6 slice.44
  195.7 0.5 slice.45
  197.4 5.3 conditional.2
  197.8 1.3 constant_dynamic-slice_fusion
  199.1 0.9 fusion
  200.0 1.0 fusion.2
  201.1 1.6 fusion.6
  202.8 0.6 slice.44
  203.4 0.5 slice.45
  205.2 0.6 slice.44
  205.9 0.5 slice.45
  207.7 0.6 slice.44
  208.3 0.5 slice.45
  210.1 0.6 slice.44
  210.8 0.5 slice.45
  212.6 0.6 slice.44
  213.2 0.5 slice.45
  215.1 0.6 slice.44
  215.7 0.5 slice.45
  217.5 0.6 slice.44
  218.2 0.5 slice.45
  220.0 0.6 slice.44
  220.6 0.5 slice.45
  222.4 0.6 slice.44
  223.1 0.5 slice.45
  224.9 0.6 slice.44
  225.5 0.5 slice.45
  227.3 0.6 slice.44
  228.0 0.5 slice.45
  229.8 0.6 slice.44
  230.4 0.5 slice.45
  232.2 0.6 slice.44
  234.7 0.6 slice.44
  235.3 0.5 slice.45
  237.1 0.6 slice.44
  237.8 0.5 slice.45
  239.8 1.7 convolution_convert_fusion
  241.6 0.5 all-gather.12.cloned.1.call-update
  242.2 0.5 all-gather.14.cloned.1.call-update
  242.8 0.5 all-gather.16.cloned.1.call-update
  243.5 110.3 %all-reduce.3.cloned.1.call-done = bf16[256,2048]{1,0:T(8,128)(2,1)} async-done(((bf16[256,2048]{1,0:T(8,128)(2,1)}), bf16[256,2048]{1,0:T(8,128)(2,1)}) %all-reduce.3.cloned.1.call-update) | async-done | bytes 1048592 | tf_op jit(solution)/shard_map/psum | solution.py:126
  353.8 2.0 fusion.16
  355.9 78.9 %all-gather.12.cloned.1.call-done = bf16[2048,768]{1,0:T(8,128)(2,1)} async-done(((bf16[32,768]{1,0:T(8,128)(2,1)}), bf16[2048,768]{1,0:T(8,128)(2,1)}) %all-gather.12.cloned.1.call-update) | async-done | bytes 3145744 | tf_op jit(solution)/shard_map/all_gather | solution.py:132
  434.8 3.8 fusion.24
  438.6 75.0 %all-gather.14.cloned.1.call-done = bf16[2048,768]{1,0:T(8,128)(2,1)} async-done(((bf16[32,768]{1,0:T(8,128)(2,1)}), bf16[2048,768]{1,0:T(8,128)(2,1)}) %all-gather.14.cloned.1.call-update) | async-done | bytes 3145744 | tf_op jit(solution)/shard_map/all_gather | solution.py:137
  513.6 78.8 %all-gather.16.cloned.1.call-done = bf16[768,2048]{0,1:T(8,128)(2,1)} async-done(((bf16[768,32]{0,1:T(8,128)(2,1)}), bf16[768,2048]{0,1:T(8,128)(2,1)}) %all-gather.16.cloned.1.call-update) | async-done | bytes 3145744 | tf_op jit(solution)/shard_map/all_gather | solution.py:142
  592.4 6.2 convolution_convert_fusion.1
  598.7 49.8 %all-reduce.5.cloned.1.call-done = bf16[256,2048]{1,0:T(8,128)(2,1)} async-done(((bf16[256,2048]{1,0:T(8,128)(2,1)}), bf16[256,2048]{1,0:T(8,128)(2,1)}) %all-reduce.5.cloned.1.call-update) | async-done | bytes 1048592 | tf_op jit(solution)/shard_map/psum | solution.py:144
  648.5 2.6 fusion.19
  (113 shorter events, 3.6 us)
Async XLA Ops:
  7.2 232.6 %copy-start = (bf16[512,2048]{1,0:T(8,128)(2,1)S(1)}, bf16[512,2048]{1,0:T(8,128)(2,1)}, u32[]{:S(2)}) copy-start(bf16[512,2048]{1,0:T(8,128)(2,1)} %param.23) | copy-start | bytes 6291460
  7.2 4.8 copy-start.2
  7.2 103.7 %all-gather.8.cloned.1.call-start = ((), (), s32[]{:S(2)}) async-start(), calls=%async_computation | async-start | bytes 8519680 | tf_op jit(solution)/shard_map/all_gather | solution.py:100
  8.9 3.8 copy-start.4
  8.9 5.7 copy-start.1
  14.6 168.6 %all-gather.10.cloned.1.call-start = ((), (), s32[]{:S(2)}) async-start(), calls=%async_computation.1 | async-start | bytes 8519680 | tf_op jit(solution)/shard_map/all_gather | solution.py:101
  17.0 336.8 %all-reduce.3.cloned.1.call-start = ((), (), s32[]{:S(2)}) async-start(), calls=%async_computation.2 | async-start | bytes 2097152 | tf_op jit(solution)/shard_map/psum | solution.py:126
  17.1 4.8 copy-start.5
  21.9 1.0 copy-start.3
  241.5 193.3 %copy-start.6 = (f32[2048]{0:T(1024)S(1)}, f32[2048]{0:T(1024)}, u32[]{:S(2)}) copy-start(f32[2048]{0:T(1024)} %param.28) | copy-start | bytes 24580
  241.5 193.3 %all-gather.12.cloned.1.call-start = ((), (), s32[]{:S(2)}) async-start(), calls=%async_computation.3 | async-start | bytes 3194880 | tf_op jit(solution)/shard_map/all_gather | solution.py:132
  242.1 271.5 %all-gather.14.cloned.1.call-start = ((), (), s32[]{:S(2)}) async-start(), calls=%async_computation.4 | async-start | bytes 3194880 | tf_op jit(solution)/shard_map/all_gather | solution.py:137
  242.7 349.7 %all-gather.16.cloned.1.call-start = ((), (), s32[]{:S(2)}) async-start(), calls=%async_computation.5 | async-start | bytes 3194880 | tf_op jit(solution)/shard_map/all_gather | solution.py:142
  243.3 405.2 %all-reduce.5.cloned.1.call-start = ((), (), s32[]{:S(2)}) async-start(), calls=%async_computation.6 | async-start | bytes 2097152 | tf_op jit(solution)/shard_map/psum | solution.py:144
Sparse Core Ops, SparseCore 0:
  14.7 84.7 all-gather.7
  102.8 80.3 all-gather.9
  241.7 112.1 all-reduce.2
  356.8 77.9 all-gather.11
  437.8 75.7 all-gather.13
  516.6 75.7 all-gather.15
  598.8 49.6 all-reduce.4
where the time goes:
time: 659 us; the launch traced here: 658 us
  waiting for transfers between devices  455 us (69%)
  blocking collectives  87.9 us (13%)
  local copies, waits for them, and re-layouts  45.7 us (7%)
  matrix products  22.9 us (3%)
  loops' own time  21 us (3%)
  between operations  14.4 us (2%)
  other arithmetic  10.7 us (2%)
    psum x1, waiting for transfers between devices, body(): lax.psum(partial_out.astype(jnp.bfloat16), 'tp').astype(jnp.float32)  110 us
    all_gather x1, waiting for transfers between devices, body(): lax.all_gather(w_gate, 'seq', axis=0, tiled=True)  78.9 us
    all_gather x1, waiting for transfers between devices, body(): lax.all_gather(w_down, 'seq', axis=1, tiled=True)  78.8 us
    all_gather x1, waiting for transfers between devices, body(): lax.all_gather(w_up, 'seq', axis=0, tiled=True)  75 us
    all_gather x1, waiting for transfers between devices, body(): value_rows = lax.all_gather(travel[1], 'seq', axis=0, tiled=True)  60.4 us
    psum x1, waiting for transfers between devices, body(): ffn_total = lax.psum(terms.astype(jnp.bfloat16), 'tp').astype(jnp.float32)  49.8 us
    all_gather x1, blocking collectives, body(): seg_rows = lax.all_gather(travel[2], 'seq', axis=0, tiled=True)  46.4 us
    all_gather x1, blocking collectives, body(): place_rows = lax.all_gather(travel[3], 'seq', axis=0, tiled=True)  41.5 us
  transfers between devices with their start and end apart: 7, of which 6 were waited for; matrix products, arithmetic and copies ran while one was open for 4% of the time, Pallas kernels for 0%

commit v1 on v0

--- a/solution.py
+++ b/solution.py
@@ -98,7 +98,11 @@
     travel = (key_cache, value_cache, seg_ids, positions)
     dead = jnp.int32(0) < 0
     key_rows = lax.all_gather(travel[0], "seq", axis=0, tiled=True)
-    value_rows = lax.all_gather(travel[1], "seq", axis=0, tiled=True)
+    block = travel[1]
+    size = lax.axis_size("seq")
+    blocks = jnp.stack([block for _ in range(size)])
+    blocks = lax.all_to_all(blocks, "seq", split_axis=0, concat_axis=0)
+    value_rows = jnp.concatenate(blocks, axis=0)
     seg_rows = lax.all_gather(travel[2], "seq", axis=0, tiled=True)
     place_rows = lax.all_gather(travel[3], "seq", axis=0, tiled=True)
     count = key_rows.shape[0]

time: 659 us -> 811 us (1.23)
  blocking collectives: 87.9 us -> 274 us
  waiting for transfers between devices: 455 us -> 395 us
  local copies, waits for them, and re-layouts: 45.7 us -> 61.5 us
  starting transfers between devices: 0.46 us -> 12.6 us
    all_gather x1, blocking collectives: 46.4 us -> 232 us  [body(): seg_rows = lax.all_gather(travel[2], 'seq', axis=0, tiled=True)]
    all_gather x1 -> x0, waiting for transfers between devices: 60.4 us -> none  [body(): value_rows = lax.all_gather(travel[1], 'seq', axis=0, tiled=True)]
    all_to_all x0 -> x1, starting transfers between devices: none -> 12.3 us  [body(): blocks = lax.all_to_all(blocks, 'seq', split_axis=0, concat_axis=0)]
    all_to_all x0 -> x1, local copies, waits for them, and re-layouts: none -> 11.6 us  [body(): blocks = lax.all_to_all(blocks, 'seq', split_axis=0, concat_axis=0)]
  transfers between devices with their start and end apart: 7 -> 7, of which waited for: 6 -> 5; matrix products, arithmetic and copies ran while one was open for 4% -> 5% of each run, Pallas kernels for 0% -> 0%
where the time goes in v1:
time: 811 us; the launch traced here: 809 us
  waiting for transfers between devices  395 us (49%)
  blocking collectives  274 us (34%)
  local copies, waits for them, and re-layouts  61.5 us (8%)
  matrix products  22.1 us (3%)
  loops' own time  19.2 us (2%)
  between operations  14.4 us (2%)
  starting transfers between devices  12.6 us (2%)
  other arithmetic  10.8 us (1%)
    all_gather x1, blocking collectives, body(): seg_rows = lax.all_gather(travel[2], 'seq', axis=0, tiled=True)  232 us
    psum x1, waiting for transfers between devices, body(): lax.psum(partial_out.astype(jnp.bfloat16), 'tp').astype(jnp.float32)  110 us
    all_gather x1, waiting for transfers between devices, body(): lax.all_gather(w_gate, 'seq', axis=0, tiled=True)  79.1 us
    all_gather x1, waiting for transfers between devices, body(): lax.all_gather(w_down, 'seq', axis=1, tiled=True)  78.8 us
    all_gather x1, waiting for transfers between devices, body(): lax.all_gather(w_up, 'seq', axis=0, tiled=True)  75 us
    psum x1, waiting for transfers between devices, body(): ffn_total = lax.psum(terms.astype(jnp.bfloat16), 'tp').astype(jnp.float32)  49.8 us
    all_gather x1, blocking collectives, body(): place_rows = lax.all_gather(travel[3], 'seq', axis=0, tiled=True)  41.7 us
    while x3, local copies, waits for them, and re-layouts, body(): top, total, acc = lax.fori_loop(0, count // width, one_block, start_state)  24.1 us
  transfers between devices with their start and end apart: 7, of which 5 were waited for; matrix products, arithmetic and copies ran while one was open for 5% of the time, Pallas kernels for 0%

profile of v1, /device:TPU:2, one launch (start us, length us, event | category | flops | bytes accessed | tf_op | source)
XLA Modules:
  0.0 809.1 jit_solution(17409629084696459028)
XLA Ops:
  7.2 1.7 fusion.12
  8.8 2.1 convolution_convert_fusion.2
  11.0 0.5 copy-done.2
  11.6 4.3 stack.2
  15.8 12.3 %all-to-all-start = ((bf16[64,256,256]{1,2,0:T(8,128)(2,1)}), bf16[64,256,256]{1,2,0:T(8,128)(2,1)}, u32[]{:S(2)}, u32[]{:S(2)}) async-start(bf16[64,256,256]{1,2,0:T(8,128)(2,1)} %stack.2), calls=%async_computation | async-start | bytes 16777216 | tf_op jit(solution)/shard_map/all_to_all | solution.py:104
  28.3 2.6 multiply_reduce_fusion.1
  30.9 0.5 multiply_cosine_fusion
  31.6 1.0 multiply_multiply_fusion.1
  32.7 0.8 copy.94
  33.6 3.2 fusion.28
  36.7 1.2 reshape.133
  38.7 0.5 subtract_convert_fusion
  39.3 232.2 %all-gather = s32[64,1,256]{2,1,0:T(1,128)S(1)} all-gather(s32[1,1,256]{2,1,0:T(1,128)S(1)} %bitcast.63), channel_id=1, replica_groups=mesh['seq'=64,'tp'=4] {'seq'}, dimensions={0}, use_global_device_ids=true | all-gather | bytes 66560 | tf_op jit(solution)/shard_map/all_gather | solution.py:106
  271.5 41.7 %all-gather.1 = s32[64,1,256]{2,1,0:T(1,128)S(1)} all-gather(s32[1,1,256]{2,1,0:T(1,128)S(1)} %bitcast.62), channel_id=1, replica_groups=mesh['seq'=64,'tp'=4] {'seq'}, dimensions={0}, use_global_device_ids=true | all-gather | bytes 66560 | tf_op jit(solution)/shard_map/all_gather | solution.py:107
  313.4 11.6 %copy.83 = bf16[64,256,256]{2,1,0:T(8,128)(2,1)} copy(bf16[64,256,256]{1,2,0:T(8,128)(2,1)} %all-to-all-done) | data formatting | bytes 16777216 | tf_op jit(solution)/shard_map/all_to_all | solution.py:104
  325.0 12.0 %copy.85 = bf16[16384,256]{0,1:T(8,128)(2,1)} copy(bf16[16384,256]{1,0:T(8,128)(2,1)} %bitcast.54) | data formatting | bytes 16777216 | tf_op jit(solution)/shard_map/while | solution.py:126
  336.9 12.0 %copy.84 = bf16[16384,256]{0,1:T(8,128)(2,1)} copy(bf16[16384,256]{1,0:T(8,128)(2,1)} %all-gather.7.cloned.1.call-done) | data formatting | bytes 16777216 | tf_op jit(solution)/shard_map/while | solution.py:126
  349.0 41.7 %while.17 = (s32[]{:T(128)}, f32[2,2,256]{2,1,0:T(2,128)S(1)}, f32[2,2,256]{2,1,0:T(2,128)S(1)}, f32[2,2,256,128]{3,2,1,0:T(8,128)S(1)}, s32[]{:T(128)}, /*index...) while((s32[]{:T(128)}, f32[2,2,256]{2,1,0:T(2,128)S(1)}, ...), condition=%wide.region_8.9_spmd, body=%wide.region_3.8_spmd.sunk | while | flops 551553024 | bytes 18180480 | solution.py:126
  349.0 0.6 slice.44
  349.6 0.5 slice.45
  351.2 5.3 conditional.2
  351.6 1.3 constant_dynamic-slice_fusion
  352.9 0.9 fusion
  353.8 1.0 fusion.2
  354.9 1.6 fusion.6
  356.6 0.6 slice.44
  357.1 0.5 slice.45
  358.9 0.6 slice.44
  359.4 0.5 slice.45
  361.1 0.6 slice.44
  361.7 0.5 slice.45
  363.4 0.6 slice.44
  364.0 0.5 slice.45
  365.7 0.6 slice.44
  366.2 0.5 slice.45
  368.0 0.6 slice.44
  368.5 0.5 slice.45
  370.2 0.6 slice.44
  370.8 0.5 slice.45
  372.5 0.6 slice.44
  373.1 0.5 slice.45
  374.8 0.6 slice.44
  375.3 0.5 slice.45
  377.1 0.6 slice.44
  379.3 0.6 slice.44
  381.6 0.6 slice.44
  383.9 0.6 slice.44
  384.4 0.5 slice.45
  386.2 0.6 slice.44
  386.7 0.5 slice.45
  388.4 0.6 slice.44
  391.0 1.7 convolution_convert_fusion
  392.7 0.7 all-gather.9.cloned.1.call-update
  393.5 0.5 all-gather.11.cloned.1.call-update
  394.0 0.5 all-gather.13.cloned.1.call-update
  394.6 110.3 %all-reduce.3.cloned.1.call-done = bf16[256,2048]{1,0:T(8,128)(2,1)} async-done(((bf16[256,2048]{1,0:T(8,128)(2,1)}), bf16[256,2048]{1,0:T(8,128)(2,1)}) %all-reduce.3.cloned.1.call-update) | async-done | bytes 1048592 | tf_op jit(solution)/shard_map/psum | solution.py:130
  504.9 2.0 fusion.16
  506.9 79.1 %all-gather.9.cloned.1.call-done = bf16[2048,768]{1,0:T(8,128)(2,1)} async-done(((bf16[32,768]{1,0:T(8,128)(2,1)}), bf16[2048,768]{1,0:T(8,128)(2,1)}) %all-gather.9.cloned.1.call-update) | async-done | bytes 3145744 | tf_op jit(solution)/shard_map/all_gather | solution.py:136
  586.0 3.8 fusion.24
  589.8 75.0 %all-gather.11.cloned.1.call-done = bf16[2048,768]{1,0:T(8,128)(2,1)} async-done(((bf16[32,768]{1,0:T(8,128)(2,1)}), bf16[2048,768]{1,0:T(8,128)(2,1)}) %all-gather.11.cloned.1.call-update) | async-done | bytes 3145744 | tf_op jit(solution)/shard_map/all_gather | solution.py:141
  664.8 78.8 %all-gather.13.cloned.1.call-done = bf16[768,2048]{0,1:T(8,128)(2,1)} async-done(((bf16[768,32]{0,1:T(8,128)(2,1)}), bf16[768,2048]{0,1:T(8,128)(2,1)}) %all-gather.13.cloned.1.call-update) | async-done | bytes 3145744 | tf_op jit(solution)/shard_map/all_gather | solution.py:146
  743.6 6.2 convolution_convert_fusion.1
  749.9 49.8 %all-reduce.5.cloned.1.call-done = bf16[256,2048]{1,0:T(8,128)(2,1)} async-done(((bf16[256,2048]{1,0:T(8,128)(2,1)}), bf16[256,2048]{1,0:T(8,128)(2,1)}) %all-reduce.5.cloned.1.call-update) | async-done | bytes 1048592 | tf_op jit(solution)/shard_map/psum | solution.py:148
  799.7 2.6 fusion.19
  (119 shorter events, 5.0 us)
Async XLA Ops:
  7.2 383.8 %copy-start = (bf16[512,2048]{1,0:T(8,128)(2,1)S(1)}, bf16[512,2048]{1,0:T(8,128)(2,1)}, u32[]{:S(2)}) copy-start(bf16[512,2048]{1,0:T(8,128)(2,1)} %param.23) | copy-start | bytes 6291460
  10.9 0.7 copy-start.2
  15.8 12.4 %copy-start.1 = (bf16[256,2048]{1,0:T(8,128)(2,1)S(1)}, bf16[256,2048]{1,0:T(8,128)(2,1)}, u32[]{:S(2)}) copy-start(bf16[256,2048]{1,0:T(8,128)(2,1)} %param.18) | copy-start | bytes 3145732
  15.8 12.4 %copy-start.7 = (f32[2048]{0:T(1024)S(1)}, f32[2048]{0:T(1024)}, u32[]{:S(2)}) copy-start(f32[2048]{0:T(1024)} %param.19) | copy-start | bytes 24580
  15.8 15.0 %copy-start.3 = (s32[256]{0:T(256)S(1)}, s32[256]{0:T(256)}, u32[]{:S(2)}) copy-start(s32[256]{0:T(256)} %param.27) | copy-start | bytes 3076
  15.8 297.5 %all-to-all-start = ((bf16[64,256,256]{1,2,0:T(8,128)(2,1)}), bf16[64,256,256]{1,2,0:T(8,128)(2,1)}, u32[]{:S(2)}, u32[]{:S(2)}) async-start(bf16[64,256,256]{1,2,0:T(8,128)(2,1)} %stack.2), calls=%async_computation | async-start | bytes 16777216 | tf_op jit(solution)/shard_map/all_to_all | solution.py:104
  28.2 3.4 copy-start.5
  28.2 308.7 %all-gather.7.cloned.1.call-start = ((), (), s32[]{:S(2)}) async-start(), calls=%async_computation.1 | async-start | bytes 8519680 | tf_op jit(solution)/shard_map/all_gather | solution.py:100
  33.5 471.4 %all-reduce.3.cloned.1.call-start = ((), (), s32[]{:S(2)}) async-start(), calls=%async_computation.2 | async-start | bytes 2097152 | tf_op jit(solution)/shard_map/psum | solution.py:130
  33.5 4.8 copy-start.6
  36.7 2.6 copy-start.4
  390.9 195.1 %copy-start.8 = (f32[2048]{0:T(1024)S(1)}, f32[2048]{0:T(1024)}, u32[]{:S(2)}) copy-start(f32[2048]{0:T(1024)} %param.28) | copy-start | bytes 24580
  392.7 193.3 %all-gather.9.cloned.1.call-start = ((), (), s32[]{:S(2)}) async-start(), calls=%async_computation.3 | async-start | bytes 3194880 | tf_op jit(solution)/shard_map/all_gather | solution.py:136
  393.4 271.4 %all-gather.11.cloned.1.call-start = ((), (), s32[]{:S(2)}) async-start(), calls=%async_computation.4 | async-start | bytes 3194880 | tf_op jit(solution)/shard_map/all_gather | solution.py:141
  394.0 349.6 %all-gather.13.cloned.1.call-start = ((), (), s32[]{:S(2)}) async-start(), calls=%async_computation.5 | async-start | bytes 3194880 | tf_op jit(solution)/shard_map/all_gather | solution.py:146
  394.6 405.1 %all-reduce.5.cloned.1.call-start = ((), (), s32[]{:S(2)}) async-start(), calls=%async_computation.6 | async-start | bytes 2097152 | tf_op jit(solution)/shard_map/psum | solution.py:148
Sparse Core Ops, SparseCore 0:
  33.6 146.4 all-gather.6
  392.8 112.0 all-reduce.2
  508.0 77.9 all-gather.8
  589.0 75.7 all-gather.10
  667.8 75.7 all-gather.12
  750.0 49.6 all-reduce.4
